TPU v7x, 32 devices: a whole 2x2x4 slice. The times are simulated.
32 devices in a mesh: fsdp: 4 (over x, core), ctx: 4 (over z), tensor: 2 (over y).
Axes of the slice: x: 2, y: 2, z: 4, core: 2. Of those that a mesh axis runs over, the one named last changes fastest.
Arguments:
- block_input: bfloat16 [4096, 2048], P(('fsdp', 'ctx')), may hold values from -6 to 6
- seq_lengths: int32 [4, 3], P('fsdp'), may hold values from 1 to 512, 1024 in all within a row
- attn_gain: bfloat16 [2048], P('fsdp'), may hold values from 0.5 to 1.5
- w_query: bfloat16 [2048, 2048], P('fsdp', 'tensor'), as said below
- w_key: bfloat16 [2048, 512], P('fsdp', 'tensor'), as said below
- w_value: bfloat16 [2048, 512], P('fsdp', 'tensor'), may hold values from -0.125 to 0.125
- w_output: bfloat16 [2048, 2048], P('tensor', 'fsdp'), may hold values from -2 to 2
- mlp_gain: bfloat16 [2048], P('fsdp'), may hold values from 0.5 to 1.5
- w_gate: bfloat16 [2048, 8192], P('fsdp', 'tensor'), may hold values from -0.125 to 0.125
- w_up: bfloat16 [2048, 8192], P('fsdp', 'tensor'), may hold values from -0.125 to 0.125
- w_down: bfloat16 [8192, 2048], P('tensor', 'fsdp'), may hold values from -0.0625 to 0.0625
- cotangent: bfloat16 [4096, 2048], P(('fsdp', 'ctx')), may hold values from -6 to 6
Outputs:
- block_output: bfloat16 [4096, 2048], P(('fsdp', 'ctx'))
- input_grad: float32 [4096, 2048], P(('fsdp', 'ctx'))
- attn_gain_grad: float32 [2048], P('fsdp')
- query_grad: float32 [2048, 2048], P('fsdp', 'tensor')
- key_grad: float32 [2048, 512], P('fsdp', 'tensor')
- value_grad: float32 [2048, 512], P('fsdp', 'tensor')
- output_grad: float32 [2048, 2048], P('tensor', 'fsdp')
- mlp_gain_grad: float32 [2048], P('fsdp')
- gate_grad: float32 [2048, 8192], P('fsdp', 'tensor')
- up_grad: float32 [2048, 8192], P('fsdp', 'tensor')
- down_grad: float32 [8192, 2048], P('tensor', 'fsdp')
Inputs may be any that keep to these rules, and one draw needn't show every extreme that they name: `seq_lengths`: each row sums to 1024, and its largest entry is exactly 512. `w_query`: a projection matrix. `w_key`: a projection matrix.
All inputs are finite; a program needn't handle non-finite values.
Results may differ from a plain program's by a relative error of at most 0.02.
Values may be sent and summed in bfloat16 or wider, within the bound.
No kernel may reach another device: no remote copies, remote signals or barrier semaphores. Data moves between devices by JAX's collectives and lax.ppermute only.
A program may use at most 320 MiB of HBM per device.

v0:
```python
import math
import jax
import jax.numpy as jnp
from jax import lax
from jax.sharding import PartitionSpec as P

HD = 64
eps_norm = 1e-05
rope_base = 500000.0


def layout(lengths_row, token_index):
    seq_ends = jnp.cumsum(lengths_row)
    passed = (token_index[:, None] >= seq_ends[None, :]).astype(jnp.int32)
    segment = jnp.sum(passed, axis=1)
    seq_start = jnp.sum(passed * lengths_row[None, :], axis=1)
    return (segment, token_index - seq_start)


def rope_tables(position):
    half_width = HD // 2
    frequency = rope_base ** (-jnp.arange(half_width, dtype=jnp.float32) / half_width)
    angles = position.astype(jnp.float32)[:, None] * frequency[None, :]
    return (jnp.cos(angles), jnp.sin(angles))


def rotate(vectors, cosine_table, sine_table, direction):
    half_width = HD // 2
    first_half = vectors[..., :half_width]
    second = vectors[..., half_width:]
    cos_rows = cosine_table[:, None, :]
    sin_rows = direction * sine_table[:, None, :]
    return jnp.concatenate(
        [first_half * cos_rows - second * sin_rows, second * cos_rows + first_half * sin_rows],
        axis=-1,
    )


def norm_forward(rows_wide):
    inv_rms = lax.rsqrt(jnp.mean(rows_wide * rows_wide, axis=-1, keepdims=True) + eps_norm)
    return (rows_wide * inv_rms, inv_rms)


def norm_backward(delta_rows, unit_rows, inv_rms, gain_weights):
    scaled = gain_weights.astype(jnp.float32)[None, :] * delta_rows
    gain_term = jnp.sum(delta_rows * unit_rows, axis=0)
    back_term = inv_rms * (
        scaled - unit_rows * jnp.mean(scaled * unit_rows, axis=-1, keepdims=True)
    )
    return (gain_term, back_term)


def head_forward(queries, key_rows, values, allowed, score_scale):
    scores = (
        jnp.einsum("tgd,sd->gts", queries, key_rows, preferred_element_type=jnp.float32)
        * score_scale
    )
    masked = jnp.where(allowed[None], scores, -1e30)
    row_max = jnp.max(masked, axis=-1, keepdims=True)
    exp_total = jnp.sum(
        jnp.where(allowed[None], jnp.exp(masked - row_max), 0.0), axis=-1, keepdims=True
    )
    log_total = row_max + jnp.log(exp_total)
    attn_prob = jnp.where(allowed[None], jnp.exp(scores - log_total), 0.0).astype(jnp.bfloat16)
    attended = jnp.einsum(
        "gts,sd->tgd", attn_prob, values, preferred_element_type=jnp.float32
    ).astype(jnp.bfloat16)
    return (attended, log_total[..., 0])


def head_backward(
    queries, key_rows, values, log_total, out_delta, inner_rows, allowed, score_scale
):
    scores = (
        jnp.einsum("tgd,sd->gts", queries, key_rows, preferred_element_type=jnp.float32)
        * score_scale
    )
    attn_prob = jnp.where(allowed[None], jnp.exp(scores - log_total[..., None]), 0.0)
    prob_delta = jnp.einsum("tgd,sd->gts", out_delta, values, preferred_element_type=jnp.float32)
    score_delta = (attn_prob * (prob_delta - inner_rows[..., None]) * score_scale).astype(
        jnp.bfloat16
    )
    query_back = jnp.einsum(
        "gts,sd->tgd", score_delta, key_rows, preferred_element_type=jnp.float32
    )
    key_back = jnp.einsum("gts,tgd->sd", score_delta, queries, preferred_element_type=jnp.float32)
    value_back = jnp.einsum(
        "gts,tgd->sd", attn_prob.astype(jnp.bfloat16), out_delta, preferred_element_type=jnp.float32
    )
    return (query_back, key_back, value_back)


def body(
    block_input,
    seq_lengths,
    attn_gain,
    w_query,
    w_key,
    w_value,
    w_output,
    mlp_gain,
    w_gate,
    w_up,
    w_down,
    cotangent,
):
    row_count = block_input.shape[0]
    group_rows = row_count * lax.axis_size("ctx")
    lengths_row = seq_lengths[0]
    score_scale = 1.0 / math.sqrt(HD)
    gain_one, query_full, key_full, value_full, output_full = (
        lax.all_gather(attn_gain, "fsdp", axis=0, tiled=True),
        lax.all_gather(w_query, "fsdp", axis=0, tiled=True),
        lax.all_gather(w_key, "fsdp", axis=0, tiled=True),
        lax.all_gather(w_value, "fsdp", axis=0, tiled=True),
        lax.all_gather(w_output, "fsdp", axis=1, tiled=True),
    )
    heads_local = query_full.shape[1] // HD
    kv_local = key_full.shape[1] // HD
    head_share = heads_local // kv_local
    local_index = lax.axis_index("ctx") * row_count + jnp.arange(row_count, dtype=jnp.int32)
    group_index = jnp.arange(group_rows, dtype=jnp.int32)
    query_segment, query_position = layout(lengths_row, local_index)
    key_segment, key_position = layout(lengths_row, group_index)
    allowed = (query_segment[:, None] == key_segment[None, :]) & (
        group_index[None, :] <= local_index[:, None]
    )
    cosine_table, sine_table = rope_tables(query_position)
    input_wide = block_input.astype(jnp.float32)
    unit_one, rstd_one = norm_forward(input_wide)
    normed_one = (unit_one * gain_one.astype(jnp.float32)[None, :]).astype(jnp.bfloat16)
    query_pre = jnp.dot(normed_one, query_full, preferred_element_type=jnp.float32).reshape(
        row_count, heads_local, HD
    )
    key_pre = jnp.dot(normed_one, key_full, preferred_element_type=jnp.float32).reshape(
        row_count, kv_local, HD
    )
    value_rows = jnp.dot(normed_one, value_full, preferred_element_type=jnp.float32).astype(
        jnp.bfloat16
    )
    query_rot = rotate(query_pre, cosine_table, sine_table, 1.0).astype(jnp.bfloat16)
    key_rot = rotate(key_pre, cosine_table, sine_table, 1.0).astype(jnp.bfloat16)
    key_all, value_all = (
        lax.all_gather(key_rot.reshape(row_count, kv_local * HD), "ctx", axis=0, tiled=True),
        lax.all_gather(value_rows, "ctx", axis=0, tiled=True),
    )
    query_heads = jnp.moveaxis(query_rot.reshape(row_count, kv_local, head_share, HD), 1, 0)
    key_heads = jnp.moveaxis(key_all.reshape(group_rows, kv_local, HD), 1, 0)
    value_heads = jnp.moveaxis(value_all.reshape(group_rows, kv_local, HD), 1, 0)
    attended, log_total = lax.map(
        lambda parts_h: head_forward(parts_h[0], parts_h[1], parts_h[2], allowed, score_scale),
        (query_heads, key_heads, value_heads),
    )
    attended_rows = jnp.moveaxis(attended, 0, 1).reshape(row_count, heads_local * HD)
    attn_part = jnp.dot(attended_rows, output_full, preferred_element_type=jnp.float32)
    residual = input_wide + lax.psum(attn_part, "tensor")
    gain_two, gate_full, up_full, down_full = (
        lax.all_gather(mlp_gain, "fsdp", axis=0, tiled=True),
        lax.all_gather(w_gate, "fsdp", axis=0, tiled=True),
        lax.all_gather(w_up, "fsdp", axis=0, tiled=True),
        lax.all_gather(w_down, "fsdp", axis=1, tiled=True),
    )
    unit_two, rstd_two = norm_forward(residual)
    normed_two = (unit_two * gain_two.astype(jnp.float32)[None, :]).astype(jnp.bfloat16)
    gate_pre = jnp.dot(normed_two, gate_full, preferred_element_type=jnp.float32)
    up_pre = jnp.dot(normed_two, up_full, preferred_element_type=jnp.float32)
    sigmoid_gate = jax.nn.sigmoid(gate_pre)
    silu_gate = gate_pre * sigmoid_gate
    activation = (silu_gate * up_pre).astype(jnp.bfloat16)
    mlp_part = jnp.dot(activation, down_full, preferred_element_type=jnp.float32)
    block_output = (
        residual + lax.psum(mlp_part.astype(jnp.bfloat16), "tensor").astype(jnp.float32)
    ).astype(jnp.bfloat16)
    act_delta = jnp.dot(cotangent, down_full.T, preferred_element_type=jnp.float32)
    silu_slope = sigmoid_gate * (1.0 + gate_pre * (1.0 - sigmoid_gate))
    gate_delta = (act_delta * up_pre * silu_slope).astype(jnp.bfloat16)
    up_delta = (act_delta * silu_gate).astype(jnp.bfloat16)
    down_term = jnp.dot(activation.T, cotangent, preferred_element_type=jnp.float32)
    gate_term = jnp.dot(normed_two.T, gate_delta, preferred_element_type=jnp.float32)
    up_term = jnp.dot(normed_two.T, up_delta, preferred_element_type=jnp.float32)
    normed_two_part = jnp.dot(
        gate_delta, gate_full.T, preferred_element_type=jnp.float32
    ) + jnp.dot(up_delta, up_full.T, preferred_element_type=jnp.float32)
    normed_two_delta = lax.psum(normed_two_part, "tensor")
    gain_two_term, residual_back = norm_backward(normed_two_delta, unit_two, rstd_two, gain_two)
    residual_delta = cotangent.astype(jnp.float32) + residual_back
    residual_low = residual_delta.astype(jnp.bfloat16)
    output_term = jnp.dot(attended_rows.T, residual_low, preferred_element_type=jnp.float32)
    attended_delta = jnp.dot(
        residual_low, output_full.T, preferred_element_type=jnp.float32
    ).astype(jnp.bfloat16)
    delta_heads = jnp.moveaxis(attended_delta.reshape(row_count, kv_local, head_share, HD), 1, 0)
    inner_rows = jnp.moveaxis(
        jnp.sum(attended.astype(jnp.float32) * delta_heads.astype(jnp.float32), axis=-1), 2, 1
    )
    query_back, key_back, value_back = lax.map(
        lambda parts_h: head_backward(
            parts_h[0],
            parts_h[1],
            parts_h[2],
            parts_h[3],
            parts_h[4],
            parts_h[5],
            allowed,
            score_scale,
        ),
        (query_heads, key_heads, value_heads, log_total, delta_heads, inner_rows),
    )
    key_sum, value_sum = (
        lax.psum_scatter(
            jnp.moveaxis(key_back, 0, 1).reshape(group_rows, kv_local * HD).astype(jnp.bfloat16),
            "ctx",
            scatter_dimension=0,
            tiled=True,
        ).astype(jnp.float32),
        lax.psum_scatter(
            jnp.moveaxis(value_back, 0, 1).reshape(group_rows, kv_local * HD).astype(jnp.bfloat16),
            "ctx",
            scatter_dimension=0,
            tiled=True,
        ).astype(jnp.float32),
    )
    query_delta = rotate(
        jnp.moveaxis(query_back, 0, 1).reshape(row_count, heads_local, HD),
        cosine_table,
        sine_table,
        -1.0,
    )
    query_delta = query_delta.reshape(row_count, heads_local * HD).astype(jnp.bfloat16)
    key_delta = rotate(key_sum.reshape(row_count, kv_local, HD), cosine_table, sine_table, -1.0)
    key_delta = key_delta.reshape(row_count, kv_local * HD).astype(jnp.bfloat16)
    value_delta = value_sum.astype(jnp.bfloat16)
    query_term = jnp.dot(normed_one.T, query_delta, preferred_element_type=jnp.float32)
    key_term = jnp.dot(normed_one.T, key_delta, preferred_element_type=jnp.float32)
    value_term = jnp.dot(normed_one.T, value_delta, preferred_element_type=jnp.float32)
    normed_one_part = (
        jnp.dot(query_delta, query_full.T, preferred_element_type=jnp.float32)
        + jnp.dot(key_delta, key_full.T, preferred_element_type=jnp.float32)
        + jnp.dot(value_delta, value_full.T, preferred_element_type=jnp.float32)
    )
    normed_one_delta = lax.psum(normed_one_part.astype(jnp.bfloat16), "tensor").astype(jnp.float32)
    gain_one_term, input_back = norm_backward(normed_one_delta, unit_one, rstd_one, gain_one)
    input_grad = residual_delta + input_back
    gain_one_s, query_s, key_s, value_s, output_s, gain_two_s, gate_s, up_s, down_s = (
        lax.psum_scatter(
            gain_one_term.astype(jnp.bfloat16), "fsdp", scatter_dimension=0, tiled=True
        ).astype(jnp.float32),
        lax.psum_scatter(
            query_term.astype(jnp.bfloat16), "fsdp", scatter_dimension=0, tiled=True
        ).astype(jnp.float32),
        lax.psum_scatter(
            key_term.astype(jnp.bfloat16), "fsdp", scatter_dimension=0, tiled=True
        ).astype(jnp.float32),
        lax.psum_scatter(
            value_term.astype(jnp.bfloat16), "fsdp", scatter_dimension=0, tiled=True
        ).astype(jnp.float32),
        lax.psum_scatter(
            output_term.astype(jnp.bfloat16), "fsdp", scatter_dimension=1, tiled=True
        ).astype(jnp.float32),
        lax.psum_scatter(
            gain_two_term.astype(jnp.bfloat16), "fsdp", scatter_dimension=0, tiled=True
        ).astype(jnp.float32),
        lax.psum_scatter(
            gate_term.astype(jnp.bfloat16), "fsdp", scatter_dimension=0, tiled=True
        ).astype(jnp.float32),
        lax.psum_scatter(
            up_term.astype(jnp.bfloat16), "fsdp", scatter_dimension=0, tiled=True
        ).astype(jnp.float32),
        lax.psum_scatter(
            down_term.astype(jnp.bfloat16), "fsdp", scatter_dimension=1, tiled=True
        ).astype(jnp.float32),
    )
    gain_one_s, query_s, key_s, value_s, output_s, gain_two_s, gate_s, up_s, down_s = (
        lax.psum(gain_one_s.astype(jnp.bfloat16), "ctx").astype(jnp.float32),
        lax.psum(query_s.astype(jnp.bfloat16), "ctx").astype(jnp.float32),
        lax.psum(key_s.astype(jnp.bfloat16), "ctx").astype(jnp.float32),
        lax.psum(value_s.astype(jnp.bfloat16), "ctx").astype(jnp.float32),
        lax.psum(output_s.astype(jnp.bfloat16), "ctx").astype(jnp.float32),
        lax.psum(gain_two_s.astype(jnp.bfloat16), "ctx").astype(jnp.float32),
        lax.psum(gate_s.astype(jnp.bfloat16), "ctx").astype(jnp.float32),
        lax.psum(up_s.astype(jnp.bfloat16), "ctx").astype(jnp.float32),
        lax.psum(down_s.astype(jnp.bfloat16), "ctx").astype(jnp.float32),
    )
    return (
        block_output,
        input_grad,
        gain_one_s,
        query_s,
        key_s,
        value_s,
        output_s,
        gain_two_s,
        gate_s,
        up_s,
        down_s,
    )


def solution(mesh):
    in_specs = (
        P(("fsdp", "ctx"), None),
        P("fsdp", None),
        P("fsdp"),
        P("fsdp", "tensor"),
        P("fsdp", "tensor"),
        P("fsdp", "tensor"),
        P("tensor", "fsdp"),
        P("fsdp"),
        P("fsdp", "tensor"),
        P("fsdp", "tensor"),
        P("tensor", "fsdp"),
        P(("fsdp", "ctx"), None),
    )
    out_specs = (
        P(("fsdp", "ctx"), None),
        P(("fsdp", "ctx"), None),
        P("fsdp"),
        P("fsdp", "tensor"),
        P("fsdp", "tensor"),
        P("fsdp", "tensor"),
        P("tensor", "fsdp"),
        P("fsdp"),
        P("fsdp", "tensor"),
        P("fsdp", "tensor"),
        P("tensor", "fsdp"),
    )
    return jax.shard_map(body, mesh=mesh, in_specs=in_specs, out_specs=out_specs, check_vma=False)
```

profile of v0, /device:TPU:0, one launch (start us, length us, event | category | flops | bytes accessed | tf_op | source)
XLA Modules:
  0.0 1844.9 jit_solution(2427764517740190867)
XLA Ops:
  30.8 16.0 all_gather.35
  49.8 15.8 all_gather.37
  65.6 17.9 all-gather.14.cloned.1.call-done
  87.7 16.2 while.28
  103.9 15.5 all-gather.16.cloned.1.call-done
  131.8 55.6 %all-reduce.11.cloned.1.call-done = f32[256,2048]{1,0:T(8,128)} async-done(((f32[256,2048]{1,0:T(8,128)}), f32[256,2048]{1,0:T(8,128)}) %all-reduce.11.cloned.1.call-update) | async-done | bytes 2097168 | tf_op jit(solution)/shard_map/psum | solution.py:156
  190.5 104.2 %all-gather.18.cloned.1.call-done = bf16[2048,4096]{1,0:T(8,128)(2,1)} async-done(((bf16[512,4096]{1,0:T(8,128)(2,1)}), bf16[2048,4096]{1,0:T(8,128)(2,1)}) %all-gather.18.cloned.1.call-update) | async-done | bytes 16777232 | tf_op jit(solution)/shard_map/all_gather | solution.py:159
  294.7 12.9 fusion.98
  307.6 94.6 %all-gather.20.cloned.1.call-done = bf16[2048,4096]{1,0:T(8,128)(2,1)} async-done(((bf16[512,4096]{1,0:T(8,128)(2,1)}), bf16[2048,4096]{1,0:T(8,128)(2,1)}) %all-gather.20.cloned.1.call-update) | async-done | bytes 16777232 | tf_op jit(solution)/shard_map/all_gather | solution.py:160
  402.2 12.9 fusion.99
  415.1 94.5 %all-gather.22.cloned.1.call-done = bf16[4096,2048]{1,0:T(8,128)(2,1)} async-done(((bf16[4096,512]{1,0:T(8,128)(2,1)}), bf16[4096,2048]{1,0:T(8,128)(2,1)}) %all-gather.22.cloned.1.call-update) | async-done | bytes 16777232 | tf_op jit(solution)/shard_map/all_gather | solution.py:161
  509.7 13.6 multiply_convert_fusion
  535.5 12.8 convolution_add_fusion.2
  548.6 62.9 %all-reduce.13.cloned.1.call-done = f32[256,2048]{1,0:T(8,128)} async-done(((f32[256,2048]{1,0:T(8,128)}), f32[256,2048]{1,0:T(8,128)}) %all-reduce.13.cloned.1.call-update) | async-done | bytes 2097168 | tf_op jit(solution)/shard_map/psum | solution.py:184
  622.4 40.6 %while.29 = (s32[]{:T(128)}, f32[4,256,4,64]{1,3,2,0:T(8,128)}, bf16[4,1024,64]{1,2,0:T(8,128)(2,1)}, bf16[4,1024,64]{1,2,0:T(8,128)(2,1)}, bf16[4,1024,64]{1,2,...) while((s32[]{:T(128)}, f32[4,256,4,64]{1,3,2,0:T(8,128)}, ...), condition=%wide.region_16.17_spmd.clone, body=%wide.region_15.16_spmd.clone.sunk | while | flops 683409408 | bytes 31890716 | solution.py:196
  663.8 21.2 %reduce-scatter.10.cloned.1.call-done = bf16[256,256]{0,1:T(8,128)(2,1)} async-done(((bf16[1024,256]{0,1:T(8,128)(2,1)}), bf16[256,256]{0,1:T(8,128)(2,1)}) %reduce-scatter.10.cloned.1.call-update) | async-done | bytes 131088 | tf_op jit(solution)/shard_map/reduce_scatter | solution.py:210
  687.7 19.7 %reduce-scatter.12.cloned.1.call-done = bf16[256,256]{0,1:T(8,128)(2,1)} async-done(((bf16[1024,256]{0,1:T(8,128)(2,1)}), bf16[256,256]{0,1:T(8,128)(2,1)}) %reduce-scatter.12.cloned.1.call-update) | async-done | bytes 131088 | tf_op jit(solution)/shard_map/reduce_scatter | solution.py:216
  775.0 32.7 %reduce-scatter.14.cloned.1.call-done = bf16[512,1024]{1,0:T(8,128)(2,1)} async-done(((bf16[2048,1024]{1,0:T(8,128)(2,1)}), bf16[512,1024]{1,0:T(8,128)(2,1)}) %reduce-scatter.14.cloned.1.call-update) | async-done | bytes 1048592 | tf_op jit(solution)/shard_map/reduce_scatter | solution.py:248
  807.8 47.4 %reduce-scatter.20.cloned.1.call-done = bf16[1024,512]{1,0:T(8,128)(2,1)} async-done(((bf16[1024,2048]{1,0:T(8,128)(2,1)}), bf16[1024,512]{1,0:T(8,128)(2,1)}) %reduce-scatter.20.cloned.1.call-update) | async-done | bytes 1048592 | tf_op jit(solution)/shard_map/reduce_scatter | solution.py:257
  855.2 127.5 %reduce-scatter.22.cloned.1.call-done = bf16[512,4096]{1,0:T(8,128)(2,1)} async-done(((bf16[2048,4096]{1,0:T(8,128)(2,1)}), bf16[512,4096]{1,0:T(8,128)(2,1)}) %reduce-scatter.22.cloned.1.call-update) | async-done | bytes 4194320 | tf_op jit(solution)/shard_map/reduce_scatter | solution.py:263
  982.7 127.5 %reduce-scatter.24.cloned.1.call-done = bf16[512,4096]{1,0:T(8,128)(2,1)} async-done(((bf16[2048,4096]{1,0:T(8,128)(2,1)}), bf16[512,4096]{1,0:T(8,128)(2,1)}) %reduce-scatter.24.cloned.1.call-update) | async-done | bytes 4194320 | tf_op jit(solution)/shard_map/reduce_scatter | solution.py:266
  1110.2 127.3 %reduce-scatter.26.cloned.1.call-done = bf16[4096,512]{1,0:T(8,128)(2,1)} async-done(((bf16[4096,2048]{1,0:T(8,128)(2,1)}), bf16[4096,512]{1,0:T(8,128)(2,1)}) %reduce-scatter.26.cloned.1.call-update) | async-done | bytes 4194320 | tf_op jit(solution)/shard_map/reduce_scatter | solution.py:269
  1239.4 64.0 %all-reduce.17.cloned.1.call-done = (bf16[256,2048]{1,0:T(8,128)(2,1)}, bf16[256,2048]{1,0:T(8,128)(2,1)}) async-done(((bf16[256,2048]{1,0:T(8,128)(2,1)}, bf16[256,2048]{1,0:T(8,128)(2,1)}), (bf16[256,2048]{1,0:T(8,128)(2,1)}, bf16[256,2048]{1,0:T(8,128)(2,1)})) %all-reduce.17.cloned.1.call-update) | async-done | bytes 2097168 | tf_op jit(solution)/shard_map/psum | solution.py:172
  1330.8 486.9 %all-reduce.15.cloned.1.call-done = (bf16[512,1024]{1,0:T(8,128)(2,1)}, bf16[512,256]{1,0:T(8,128)(2,1)}, bf16[512,256]{1,0:T(8,128)(2,1)}, bf16[1024,512]{1,0:T...) async-done(((bf16[512,1024]{1,0:T(8,128)(2,1)}, bf16[512,256]{1,0:T(8,128)(2,1)}, bf16[512,256]{1,0:T(8,128)(2,1)}, ...) | async-done | bytes 15204368 | tf_op jit(solution)/shard_map/psum | solution.py:275
  (252 shorter events, 245.0 us)
Async XLA Ops:
  7.2 21.9 %all-gather.10.cloned.1.call-start = ((), (), s32[]{:S(2)}) async-start(), calls=%async_computation.9 | async-start | bytes 1310720 | tf_op jit(solution)/shard_map/all_gather | solution.py:115
  7.9 39.9 %all-gather.12.cloned.1.call-start = ((), (), s32[]{:S(2)}) async-start(), calls=%async_computation.10 | async-start | bytes 1310720 | tf_op jit(solution)/shard_map/all_gather | solution.py:114
  8.7 74.8 %all-gather.14.cloned.1.call-start = ((), (), s32[]{:S(2)}) async-start(), calls=%async_computation.11 | async-start | bytes 5242880 | tf_op jit(solution)/shard_map/all_gather | solution.py:113
  9.4 110.0 %all-gather.16.cloned.1.call-start = ((), (), s32[]{:S(2)}) async-start(), calls=%async_computation.12 | async-start | bytes 5242880 | tf_op jit(solution)/shard_map/all_gather | solution.py:116
  10.0 177.3 %all-reduce.11.cloned.1.call-start = ((), (), s32[]{:S(2)}) async-start(), calls=%async_computation.13 | async-start | bytes 4194304 | tf_op jit(solution)/shard_map/psum | solution.py:156
  103.9 20.3 %copy-start.3 = (bf16[4,1024,64]{1,2,0:T(8,128)(2,1)}, bf16[4,1024,64]{1,2,0:T(8,128)(2,1)S(1)}, u32[]{:S(2)}) copy-start(bf16[4,1024,64]{1,2,0:T(8,128)(2,1)S(1)} %get-tuple-element.519) | copy-start | bytes 1572868
  103.9 20.3 %copy-start.4 = (bf16[4,256,4,64]{1,3,2,0:T(8,128)(2,1)}, bf16[4,256,4,64]{1,3,2,0:T(8,128)(2,1)S(1)}, u32[]{:S(2)}) copy-start(bf16[4,256,4,64]{1,3,2,0:T(8,128)(2,1)S(1)} %get-tuple-element.520) | copy-start | bytes 1572868
  103.9 20.3 %copy-start.9 = (bf16[4,256,4,64]{1,3,2,0:T(8,128)(2,1)}, bf16[4,256,4,64]{1,3,2,0:T(8,128)(2,1)S(1)}, u32[]{:S(2)}) copy-start(bf16[4,256,4,64]{1,3,2,0:T(8,128)(2,1)S(1)} %get-tuple-element.108) | copy-start | bytes 1572868
  124.2 170.5 %all-gather.18.cloned.1.call-start = ((), (), s32[]{:S(2)}) async-start(), calls=%async_computation.14 | async-start | bytes 20971520 | tf_op jit(solution)/shard_map/all_gather | solution.py:159
  124.8 277.4 %all-gather.20.cloned.1.call-start = ((), (), s32[]{:S(2)}) async-start(), calls=%async_computation.15 | async-start | bytes 20971520 | tf_op jit(solution)/shard_map/all_gather | solution.py:160
  125.5 384.1 %all-gather.22.cloned.1.call-start = ((), (), s32[]{:S(2)}) async-start(), calls=%async_computation.16 | async-start | bytes 20971520 | tf_op jit(solution)/shard_map/all_gather | solution.py:161
  126.3 485.1 %all-reduce.13.cloned.1.call-start = ((), (), s32[]{:S(2)}) async-start(), calls=%async_computation.17 | async-start | bytes 4194304 | tf_op jit(solution)/shard_map/psum | solution.py:184
  548.3 136.7 %reduce-scatter.10.cloned.1.call-start = ((), (), s32[]{:S(2)}) async-start(), calls=%async_computation.18 | async-start | bytes 655360 | tf_op jit(solution)/shard_map/reduce_scatter | solution.py:210
  663.0 44.4 %reduce-scatter.12.cloned.1.call-start = ((), (), s32[]{:S(2)}) async-start(), calls=%async_computation.19 | async-start | bytes 655360 | tf_op jit(solution)/shard_map/reduce_scatter | solution.py:216
  663.8 111.2 %reduce-scatter.16.cloned.1.call-start = ((), (), s32[]{:S(2)}) async-start(), calls=%async_computation.21 | async-start | bytes 1310720 | tf_op jit(solution)/shard_map/reduce_scatter | solution.py:251
  687.7 87.4 %reduce-scatter.18.cloned.1.call-start = ((), (), s32[]{:S(2)}) async-start(), calls=%async_computation.22 | async-start | bytes 1310720 | tf_op jit(solution)/shard_map/reduce_scatter | solution.py:254
  709.9 97.9 %reduce-scatter.14.cloned.1.call-start = ((), (), s32[]{:S(2)}) async-start(), calls=%async_computation.20 | async-start | bytes 5242880 | tf_op jit(solution)/shard_map/reduce_scatter | solution.py:248
  715.6 139.5 %reduce-scatter.20.cloned.1.call-start = ((), (), s32[]{:S(2)}) async-start(), calls=%async_computation.23 | async-start | bytes 5242880 | tf_op jit(solution)/shard_map/reduce_scatter | solution.py:257
  720.8 261.9 %reduce-scatter.22.cloned.1.call-start = ((), (), s32[]{:S(2)}) async-start(), calls=%async_computation.24 | async-start | bytes 20971520 | tf_op jit(solution)/shard_map/reduce_scatter | solution.py:263
  733.3 376.8 %reduce-scatter.24.cloned.1.call-start = ((), (), s32[]{:S(2)}) async-start(), calls=%async_computation.25 | async-start | bytes 20971520 | tf_op jit(solution)/shard_map/reduce_scatter | solution.py:266
  746.0 491.5 %reduce-scatter.26.cloned.1.call-start = ((), (), s32[]{:S(2)}) async-start(), calls=%async_computation.26 | async-start | bytes 20971520 | tf_op jit(solution)/shard_map/reduce_scatter | solution.py:269
  758.5 545.0 %all-reduce.17.cloned.1.call-start = ((), (), s32[]{:S(2)}) async-start(), calls=%async_computation.28 | async-start | bytes 4194304 | tf_op jit(solution)/shard_map/psum | solution.py:172
  758.5 12.1 copy-start.11
  774.9 1042.8 %all-reduce.15.cloned.1.call-start = ((), (), s32[]{:S(2)}) async-start(), calls=%async_computation.27 | async-start | bytes 30408704 | tf_op jit(solution)/shard_map/psum | solution.py:275
  (40 other events, 112.2 us)
Sparse Core Ops, SparseCore 0:
  9.6 19.4 all-gather.9
  30.6 16.7 all-gather.11
  49.0 34.4 all-gather.13
  84.9 34.4 all-gather.15
  124.3 62.9 all-reduce.10
  188.8 105.8 all-gather.17
  296.2 105.8 all-gather.19
  403.7 105.8 all-gather.21
  548.4 62.9 all-reduce.12
  663.2 21.8 reduce-scatter.9
  687.3 20.0 reduce-scatter.11
  709.8 22.9 reduce-scatter.15
  735.4 24.8 reduce-scatter.17
  763.2 44.5 reduce-scatter.13
  810.7 44.3 reduce-scatter.19
  857.6 125.0 reduce-scatter.21
  985.1 125.0 reduce-scatter.23
  1112.6 124.8 reduce-scatter.25
  1240.5 62.9 all-reduce.16
  1306.8 510.9 all-reduce.14
where the time goes:
time: 1850 us; the launch traced here: 1840 us
  waiting for transfers between devices  1520 us (82%)
  matrix products  191 us (10%)
  blocking collectives  62.5 us (3%)
  other arithmetic  45.1 us (2%)
    psum x1, waiting for transfers between devices, body(): lax.psum(query_s.astype(jnp.bfloat16), 'ctx').astype(jnp.float32)  487 us
    reduce_scatter x1, waiting for transfers between devices, body(): lax.psum_scatter(gate_term.astype(jnp.bfloat16), 'fsdp', scatter_dimensio...  128 us
    reduce_scatter x1, waiting for transfers between devices, body(): lax.psum_scatter(up_term.astype(jnp.bfloat16), 'fsdp', scatter_dimension=...  128 us
    reduce_scatter x1, waiting for transfers between devices, body(): lax.psum_scatter(down_term.astype(jnp.bfloat16), 'fsdp', scatter_dimensio...  127 us
    all_gather x1, waiting for transfers between devices, body(): lax.all_gather(w_gate, 'fsdp', axis=0, tiled=True)  104 us
    all_gather x1, waiting for transfers between devices, body(): lax.all_gather(w_up, 'fsdp', axis=0, tiled=True)  94.6 us
    all_gather x1, waiting for transfers between devices, body(): lax.all_gather(w_down, 'fsdp', axis=1, tiled=True)  94.5 us
    psum x1, waiting for transfers between devices, body(): lax.psum(mlp_part.astype(jnp.bfloat16), 'tensor').astype(jnp.float32)  64 us
  transfers between devices with their start and end apart: 20, of which 17 were waited for; matrix products, arithmetic and copies ran while one was open for 7% of the time, Pallas kernels for 0%

commit v1 on v0

--- a/solution.py
+++ b/solution.py
@@ -7,6 +7,17 @@
 HD = 64
 eps_norm = 1e-05
 rope_base = 500000.0
+
+
+def gather_around(array, axis, dim):
+    ways = lax.axis_size(axis)
+    pieces = [array]
+    for far in range(1, ways):
+        pieces.append(
+            lax.ppermute(pieces[far - 1], axis, [(d, (d - 1) % ways) for d in range(ways)])
+        )
+    line = jnp.concatenate(pieces, axis=dim)
+    return jnp.roll(line, lax.axis_index(axis) * array.shape[dim], axis=dim)
 
 
 def layout(lengths_row, token_index):
@@ -156,7 +167,7 @@
     residual = input_wide + lax.psum(attn_part, "tensor")
     gain_two, gate_full, up_full, down_full = (
         lax.all_gather(mlp_gain, "fsdp", axis=0, tiled=True),
-        lax.all_gather(w_gate, "fsdp", axis=0, tiled=True),
+        gather_around(w_gate, "fsdp", 0),
         lax.all_gather(w_up, "fsdp", axis=0, tiled=True),
         lax.all_gather(w_down, "fsdp", axis=1, tiled=True),
     )

time: 1850 us -> 1810 us (0.978)
  waiting for transfers between devices: 1520 us -> 1330 us
  blocking collectives: 62.5 us -> 161 us
  local copies, waits for them, and re-layouts: 12.1 us -> 46.6 us
    ppermute x0 -> x3, waiting for transfers between devices: none -> 136 us  [gather_around(): lax.ppermute(pieces[far - 1], axis, [(d, (d - 1) % ways) for d in range(w...]
    all_gather x1 -> x0, waiting for transfers between devices: 104 us -> none  [body(): lax.all_gather(w_gate, 'fsdp', axis=0, tiled=True)]
    all_gather x1, blocking collectives: 5.4 us -> 104 us  [body(): lax.all_gather(mlp_gain, 'fsdp', axis=0, tiled=True)]
    all_gather x1, waiting for transfers between devices: 94.6 us -> 0.01 us  [body(): lax.all_gather(w_up, 'fsdp', axis=0, tiled=True)]
    all_gather x1, waiting for transfers between devices: 94.5 us -> 31.2 us  [body(): lax.all_gather(w_down, 'fsdp', axis=1, tiled=True)]
    psum x1, waiting for transfers between devices: 55.6 us -> 0.01 us  [body(): residual = input_wide + lax.psum(attn_part, 'tensor')]
    unnamed x53 -> x64, local copies, waits for them, and re-layouts: 5.75 us -> 35.6 us
  transfers between devices with their start and end apart: 20 -> 22, of which waited for: 17 -> 16; matrix products, arithmetic and copies ran while one was open for 7% -> 8% of each run, Pallas kernels for 0% -> 0%
where the time goes in v1:
time: 1810 us; the launch traced here: 1800 us
  waiting for transfers between devices  1330 us (73%)
  matrix products  193 us (11%)
  blocking collectives  161 us (9%)
  other arithmetic  48.7 us (3%)
  local copies, waits for them, and re-layouts  46.6 us (3%)
    psum x1, waiting for transfers between devices, body(): lax.psum(query_s.astype(jnp.bfloat16), 'ctx').astype(jnp.float32)  487 us
    ppermute x3, waiting for transfers between devices, gather_around(): lax.ppermute(pieces[far - 1], axis, [(d, (d - 1) % ways) for d in range(w...  136 us
    reduce_scatter x1, waiting for transfers between devices, body(): lax.psum_scatter(up_term.astype(jnp.bfloat16), 'fsdp', scatter_dimension=...  128 us
    reduce_scatter x1, waiting for transfers between devices, body(): lax.psum_scatter(gate_term.astype(jnp.bfloat16), 'fsdp', scatter_dimensio...  128 us
    reduce_scatter x1, waiting for transfers between devices, body(): lax.psum_scatter(down_term.astype(jnp.bfloat16), 'fsdp', scatter_dimensio...  127 us
    all_gather x1, blocking collectives, body(): lax.all_gather(mlp_gain, 'fsdp', axis=0, tiled=True)  104 us
    psum x1, waiting for transfers between devices, body(): lax.psum(mlp_part.astype(jnp.bfloat16), 'tensor').astype(jnp.float32)  63.9 us
    psum x1, waiting for transfers between devices, body(): normed_two_delta = lax.psum(normed_two_part, 'tensor')  62.9 us
  transfers between devices with their start and end apart: 22, of which 16 were waited for; matrix products, arithmetic and copies ran while one was open for 8% of the time, Pallas kernels for 0%

profile of v1, /device:TPU:0, one launch (start us, length us, event | category | flops | bytes accessed | tf_op | source)
XLA Modules:
  0.0 1803.2 jit_solution(10201216505903942282)
XLA Ops:
  31.3 16.0 all_gather.34
  49.0 16.0 all_gather.32
  66.1 17.3 all-gather.13.cloned.1.call-done
  87.6 16.2 while.28
  103.8 15.5 all-gather.15.cloned.1.call-done
  125.7 46.3 %collective-permute-done = bf16[512,4096]{1,0:T(8,128)(2,1)S(1)} collective-permute-done((bf16[512,4096]{1,0:T(8,128)(2,1)}, bf16[512,4096]{1,0:T(8,128)(2,1)S(1)}, u32[]{:S(2)}, u32[]{:S(2)}) %collective-permute-start) | collective-permute-done | bytes 4194336 | tf_op jit(solution)/shard_map/ppermute | solution.py:17
  176.3 89.9 %collective-permute-done.1 = bf16[512,4096]{1,0:T(8,128)(2,1)} collective-permute-done((bf16[512,4096]{1,0:T(8,128)(2,1)S(1)}, bf16[512,4096]{1,0:T(8,128)(2,1)}, u32[]{:S(2)}, u32[]{:S(2)}) %collective-permute-start.1) | collective-permute-done | bytes 4194336 | tf_op jit(solution)/shard_map/ppermute | solution.py:17
  268.5 103.8 %all-gather.1 = bf16[4,1,512]{2,1,0:T(2,128)(2,1)S(1)} all-gather(bf16[1,1,512]{2,1,0:T(2,128)(2,1)S(1)} %reshape.251), channel_id=1, replica_groups=mesh['fsdp'=4,'ctx'=4,'tensor'=2] {'fsdp'}, dimensions={0}, use_global_device_ids=true | all-gather | bytes 5120 | tf_op jit(solution)/shard_map/all_gather | solution.py:169
  407.5 12.6 fusion.107
  420.1 31.2 %all-gather.19.cloned.1.call-done = bf16[4096,2048]{1,0:T(8,128)(2,1)} async-done(((bf16[4096,512]{1,0:T(8,128)(2,1)}), bf16[4096,2048]{1,0:T(8,128)(2,1)}) %all-gather.19.cloned.1.call-update) | async-done | bytes 16777232 | tf_op jit(solution)/shard_map/all_gather | solution.py:172
  451.3 12.6 fusion.108
  464.0 13.9 multiply_convert_fusion.1
  490.1 12.8 fusion.81
  503.2 62.9 %all-reduce.13.cloned.1.call-done = f32[256,2048]{1,0:T(8,128)} async-done(((f32[256,2048]{1,0:T(8,128)}), f32[256,2048]{1,0:T(8,128)}) %all-reduce.13.cloned.1.call-update) | async-done | bytes 2097168 | tf_op jit(solution)/shard_map/psum | solution.py:195
  576.9 43.0 %while.29 = (s32[]{:T(128)}, f32[4,256,4,64]{1,3,2,0:T(8,128)}, bf16[4,1024,64]{1,2,0:T(8,128)(2,1)}, bf16[4,1024,64]{1,2,0:T(8,128)(2,1)}, bf16[4,1024,64]{1,2,...) while((s32[]{:T(128)}, f32[4,256,4,64]{1,3,2,0:T(8,128)}, ...), condition=%wide.region_16.17_spmd.clone, body=%wide.region_15.16_spmd.clone.sunk | while | flops 683409408 | bytes 27696348 | solution.py:207
  620.5 21.4 %reduce-scatter.10.cloned.1.call-done = bf16[256,256]{0,1:T(8,128)(2,1)} async-done(((bf16[1024,256]{0,1:T(8,128)(2,1)}), bf16[256,256]{0,1:T(8,128)(2,1)}) %reduce-scatter.10.cloned.1.call-update) | async-done | bytes 131088 | tf_op jit(solution)/shard_map/reduce_scatter | solution.py:221
  644.6 20.2 %reduce-scatter.12.cloned.1.call-done = bf16[256,256]{0,1:T(8,128)(2,1)} async-done(((bf16[1024,256]{0,1:T(8,128)(2,1)}), bf16[256,256]{0,1:T(8,128)(2,1)}) %reduce-scatter.12.cloned.1.call-update) | async-done | bytes 131088 | tf_op jit(solution)/shard_map/reduce_scatter | solution.py:227
  732.4 32.8 %reduce-scatter.20.cloned.1.call-done = bf16[1024,512]{1,0:T(8,128)(2,1)} async-done(((bf16[1024,2048]{1,0:T(8,128)(2,1)}), bf16[1024,512]{1,0:T(8,128)(2,1)}) %reduce-scatter.20.cloned.1.call-update) | async-done | bytes 1048592 | tf_op jit(solution)/shard_map/reduce_scatter | solution.py:268
  765.2 47.6 %reduce-scatter.14.cloned.1.call-done = bf16[512,1024]{1,0:T(8,128)(2,1)} async-done(((bf16[2048,1024]{1,0:T(8,128)(2,1)}), bf16[512,1024]{1,0:T(8,128)(2,1)}) %reduce-scatter.14.cloned.1.call-update) | async-done | bytes 1048592 | tf_op jit(solution)/shard_map/reduce_scatter | solution.py:259
  812.8 127.5 %reduce-scatter.22.cloned.1.call-done = bf16[512,4096]{1,0:T(8,128)(2,1)} async-done(((bf16[2048,4096]{1,0:T(8,128)(2,1)}), bf16[512,4096]{1,0:T(8,128)(2,1)}) %reduce-scatter.22.cloned.1.call-update) | async-done | bytes 4194320 | tf_op jit(solution)/shard_map/reduce_scatter | solution.py:274
  940.3 127.5 %reduce-scatter.24.cloned.1.call-done = bf16[512,4096]{1,0:T(8,128)(2,1)} async-done(((bf16[2048,4096]{1,0:T(8,128)(2,1)}), bf16[512,4096]{1,0:T(8,128)(2,1)}) %reduce-scatter.24.cloned.1.call-update) | async-done | bytes 4194320 | tf_op jit(solution)/shard_map/reduce_scatter | solution.py:277
  1067.8 127.3 %reduce-scatter.26.cloned.1.call-done = bf16[4096,512]{1,0:T(8,128)(2,1)} async-done(((bf16[4096,2048]{1,0:T(8,128)(2,1)}), bf16[4096,512]{1,0:T(8,128)(2,1)}) %reduce-scatter.26.cloned.1.call-update) | async-done | bytes 4194320 | tf_op jit(solution)/shard_map/reduce_scatter | solution.py:280
  1197.0 63.9 %all-reduce.17.cloned.1.call-done = (bf16[256,2048]{1,0:T(8,128)(2,1)}, bf16[256,2048]{1,0:T(8,128)(2,1)}) async-done(((bf16[256,2048]{1,0:T(8,128)(2,1)}, bf16[256,2048]{1,0:T(8,128)(2,1)}), (bf16[256,2048]{1,0:T(8,128)(2,1)}, bf16[256,2048]{1,0:T(8,128)(2,1)})) %all-reduce.17.cloned.1.call-update) | async-done | bytes 2097168 | tf_op jit(solution)/shard_map/psum | solution.py:183
  1288.2 487.1 %all-reduce.15.cloned.1.call-done = (bf16[512,1024]{1,0:T(8,128)(2,1)}, bf16[512,256]{1,0:T(8,128)(2,1)}, bf16[512,256]{1,0:T(8,128)(2,1)}, bf16[1024,512]{1,0:T...) async-done(((bf16[512,1024]{1,0:T(8,128)(2,1)}, bf16[512,256]{1,0:T(8,128)(2,1)}, bf16[512,256]{1,0:T(8,128)(2,1)}, ...) | async-done | bytes 15204368 | tf_op jit(solution)/shard_map/psum | solution.py:286
  (251 shorter events, 281.0 us)
Async XLA Ops:
  7.2 40.1 %copy-start = (bf16[256,2048]{1,0:T(8,128)(2,1)S(1)}, bf16[256,2048]{1,0:T(8,128)(2,1)}, u32[]{:S(2)}) copy-start(bf16[256,2048]{1,0:T(8,128)(2,1)} %param.16) | copy-start | bytes 3145732
  7.2 21.8 %all-gather.11.cloned.1.call-start = ((), (), s32[]{:S(2)}) async-start(), calls=%async_computation.10 | async-start | bytes 1310720 | tf_op jit(solution)/shard_map/all_gather | solution.py:125
  7.9 39.4 %all-gather.9.cloned.1.call-start = ((), (), s32[]{:S(2)}) async-start(), calls=%async_computation.9 | async-start | bytes 1310720 | tf_op jit(solution)/shard_map/all_gather | solution.py:126
  8.7 74.7 %all-gather.13.cloned.1.call-start = ((), (), s32[]{:S(2)}) async-start(), calls=%async_computation.11 | async-start | bytes 5242880 | tf_op jit(solution)/shard_map/all_gather | solution.py:124
  9.4 109.9 %all-gather.15.cloned.1.call-start = ((), (), s32[]{:S(2)}) async-start(), calls=%async_computation.12 | async-start | bytes 5242880 | tf_op jit(solution)/shard_map/all_gather | solution.py:127
  10.0 369.4 %all-reduce.11.cloned.1.call-start = ((), (), s32[]{:S(2)}) async-start(), calls=%async_computation.13 | async-start | bytes 4194304 | tf_op jit(solution)/shard_map/psum | solution.py:167
  124.1 144.4 %copy-start.25 = (bf16[512]{0:T(512)(128)(2,1)S(1)}, bf16[512]{0:T(512)(128)(2,1)}, u32[]{:S(2)}) copy-start(bf16[512]{0:T(512)(128)(2,1)} %param.23) | copy-start | bytes 3076
  124.1 283.4 %all-gather.17.cloned.1.call-start = ((), (), s32[]{:S(2)}) async-start(), calls=%async_computation.14 | async-start | bytes 20971520 | tf_op jit(solution)/shard_map/all_gather | solution.py:171
  124.7 326.7 %all-gather.19.cloned.1.call-start = ((), (), s32[]{:S(2)}) async-start(), calls=%async_computation.15 | async-start | bytes 20971520 | tf_op jit(solution)/shard_map/all_gather | solution.py:172
  125.4 440.7 %all-reduce.13.cloned.1.call-start = ((), (), s32[]{:S(2)}) async-start(), calls=%async_computation.16 | async-start | bytes 4194304 | tf_op jit(solution)/shard_map/psum | solution.py:195
  125.5 46.6 %collective-permute-start = (bf16[512,4096]{1,0:T(8,128)(2,1)}, bf16[512,4096]{1,0:T(8,128)(2,1)S(1)}, u32[]{:S(2)}, u32[]{:S(2)}) collective-permute-start(bf16[512,4096]{1,0:T(8,128)(2,1)} %param.24), channel_id=1, source_target_pairs={{0,24},{8,0},{16,8},{24,16},{1,25},{9,1},{17,9},{25,17},{2,26},{10... | collective-permute-start | bytes 12582920 | tf_op jit(solution)/shard_map/ppermute | solution.py:17
  174.1 92.1 %collective-permute-start.1 = (bf16[512,4096]{1,0:T(8,128)(2,1)S(1)}, bf16[512,4096]{1,0:T(8,128)(2,1)}, u32[]{:S(2)}, u32[]{:S(2)}) collective-permute-start(bf16[512,4096]{1,0:T(8,128)(2,1)S(1)} %collective-permute-done), channel_id=1, source_target_pairs={{0,24},{8,0},{16,8},{24,16},{1,25},{9,1},{17,9},{25,17},{2,26},{10... | collective-permute-start | bytes 12582920 | tf_op jit(solution)/shard_map/ppermute | solution.py:17
  266.2 121.2 %collective-permute-start.2 = (bf16[512,4096]{1,0:T(8,128)(2,1)}, bf16[512,4096]{1,0:T(8,128)(2,1)}, u32[]{:S(2)}, u32[]{:S(2)}) collective-permute-start(bf16[512,4096]{1,0:T(8,128)(2,1)} %collective-permute-done.1), channel_id=1, source_target_pairs={{0,24},{8,0},{16,8},{24,16},{1,25},{9,1},{17,9},{25,17},{2,26},{10... | collective-permute-start | bytes 12582920 | tf_op jit(solution)/shard_map/ppermute | solution.py:17
  503.0 138.9 %reduce-scatter.10.cloned.1.call-start = ((), (), s32[]{:S(2)}) async-start(), calls=%async_computation.17 | async-start | bytes 655360 | tf_op jit(solution)/shard_map/reduce_scatter | solution.py:221
  619.9 44.8 %reduce-scatter.12.cloned.1.call-start = ((), (), s32[]{:S(2)}) async-start(), calls=%async_computation.18 | async-start | bytes 655360 | tf_op jit(solution)/shard_map/reduce_scatter | solution.py:227
  620.5 111.9 %reduce-scatter.16.cloned.1.call-start = ((), (), s32[]{:S(2)}) async-start(), calls=%async_computation.20 | async-start | bytes 1310720 | tf_op jit(solution)/shard_map/reduce_scatter | solution.py:262
  644.5 87.8 %reduce-scatter.18.cloned.1.call-start = ((), (), s32[]{:S(2)}) async-start(), calls=%async_computation.21 | async-start | bytes 1310720 | tf_op jit(solution)/shard_map/reduce_scatter | solution.py:265
  667.2 97.9 %reduce-scatter.20.cloned.1.call-start = ((), (), s32[]{:S(2)}) async-start(), calls=%async_computation.22 | async-start | bytes 5242880 | tf_op jit(solution)/shard_map/reduce_scatter | solution.py:268
  672.4 140.4 %reduce-scatter.14.cloned.1.call-start = ((), (), s32[]{:S(2)}) async-start(), calls=%async_computation.19 | async-start | bytes 5242880 | tf_op jit(solution)/shard_map/reduce_scatter | solution.py:259
  678.1 262.1 %reduce-scatter.22.cloned.1.call-start = ((), (), s32[]{:S(2)}) async-start(), calls=%async_computation.23 | async-start | bytes 20971520 | tf_op jit(solution)/shard_map/reduce_scatter | solution.py:274
  690.6 377.1 %reduce-scatter.24.cloned.1.call-start = ((), (), s32[]{:S(2)}) async-start(), calls=%async_computation.24 | async-start | bytes 20971520 | tf_op jit(solution)/shard_map/reduce_scatter | solution.py:277
  703.3 491.8 %reduce-scatter.26.cloned.1.call-start = ((), (), s32[]{:S(2)}) async-start(), calls=%async_computation.25 | async-start | bytes 20971520 | tf_op jit(solution)/shard_map/reduce_scatter | solution.py:280
  715.8 545.1 %all-reduce.17.cloned.1.call-start = ((), (), s32[]{:S(2)}) async-start(), calls=%async_computation.27 | async-start | bytes 4194304 | tf_op jit(solution)/shard_map/psum | solution.py:183
  732.3 1043.1 %all-reduce.15.cloned.1.call-start = ((), (), s32[]{:S(2)}) async-start(), calls=%async_computation.26 | async-start | bytes 30408704 | tf_op jit(solution)/shard_map/psum | solution.py:286
  (36 other events, 174.2 us)
Sparse Core Ops, SparseCore 0:
  9.6 19.4 all-gather.10
  30.6 16.6 all-gather.8
  48.9 34.4 all-gather.12
  84.8 34.4 all-gather.14
  124.2 62.9 all-reduce.10
  188.6 149.1 all-gather.16
  339.3 111.9 all-gather.18
  503.1 62.9 all-reduce.12
  620.0 21.8 reduce-scatter.9
  644.6 20.1 reduce-scatter.11
  667.3 23.0 reduce-scatter.15
  692.8 24.7 reduce-scatter.17
  720.7 44.4 reduce-scatter.19
  768.1 44.5 reduce-scatter.13
  815.2 125.0 reduce-scatter.21
  942.7 125.0 reduce-scatter.23
  1070.2 124.8 reduce-scatter.25
  1197.9 62.9 all-reduce.16
  1264.3 510.9 all-reduce.14
